TPU v7x, 128 devices: a whole 4x4x4 slice. The times are simulated.
128 devices in a mesh: dp: 8 (over z, core), mp: 16 (over x, y).
Axes of the slice: x: 4, y: 4, z: 4, core: 2. Of those that a mesh axis runs over, the one named last changes fastest.
Arguments:
- activations: bfloat16 [16384, 5120], P(('dp', 'mp')), may hold values from -10 to 10
- cotangent: bfloat16 [16384, 5120], P('dp', 'mp'), may hold values from -1 to 1
- master_weights: float32 [5120, 5120], P('dp', 'mp'), may hold values from -32 to 32
- first_moment: float32 [5120, 5120], P('dp', 'mp'), may hold values from -1 to 1
- second_moment: float32 [5120, 5120], P('dp', 'mp'), may hold values from 0.25 to 4
- step_count: int32 [1], replicated, may hold values from 1 to 23
- language_ids: int32 [1], replicated, may hold values from 0 to 7
- language_rates: float32 [8], replicated, may hold values from 0.25 to 2
Outputs:
- new_master: float32 [5120, 5120], P('dp', 'mp')
- new_first: float32 [5120, 5120], P('dp', 'mp')
- new_second: float32 [5120, 5120], P('dp', 'mp')
- new_weights: bfloat16 [5120, 5120], P(None, 'mp')
All inputs are finite; a program needn't handle non-finite values.
Results may differ from a plain program's by a relative error of at most 0.0004.
Values may be sent and summed in bfloat16 or wider, within the bound.
No kernel may reach another device: no remote copies, remote signals or barrier semaphores. Data moves between devices by JAX's collectives and lax.ppermute only.
A program may use at most 128 MiB of HBM per device.

v0:
```python
import jax
import jax.numpy as jnp
from jax import lax
from jax.sharding import PartitionSpec as P

beta_one = 0.9
beta_two = 0.999
epsilon = 1e-06
decay_weight = 0.1
base_rate = 0.25


def on_device(
    activations,
    cotangent,
    master_weights,
    first_moment,
    second_moment,
    step_count,
    language_ids,
    language_rates,
):
    gathered = lax.all_gather(activations, "mp", axis=0, tiled=True)
    gradient = lax.psum_scatter(
        lax.dot_general(
            gathered, cotangent, (((0,), (0,)), ((), ())), preferred_element_type=jnp.float32
        ),
        "dp",
        scatter_dimension=0,
        tiled=True,
    )
    steps_done = step_count[0].astype(jnp.float32)
    corr_one = 1.0 - jnp.power(jnp.float32(beta_one), steps_done)
    corr_two = 1.0 - jnp.power(jnp.float32(beta_two), steps_done)
    new_first = beta_one * first_moment + (1.0 - beta_one) * gradient
    new_second = beta_two * second_moment + (1.0 - beta_two) * gradient * gradient
    update = (
        new_first / corr_one / (jnp.sqrt(new_second / corr_two) + epsilon)
        + decay_weight * master_weights
    )
    weight_sq, update_sq = lax.psum(
        (jnp.sum(master_weights * master_weights), jnp.sum(update * update)), ("dp", "mp")
    )
    trust = jnp.sqrt(weight_sq) / jnp.sqrt(update_sq)
    picked = jnp.arange(language_rates.shape[0], dtype=jnp.int32) == language_ids[0]
    rate = base_rate * jnp.sum(jnp.where(picked, language_rates, jnp.float32(0.0)))
    new_master = master_weights - rate * trust * update
    new_weights = lax.all_gather(new_master.astype(jnp.bfloat16), "dp", axis=0, tiled=True)
    return (new_master, new_first, new_second, new_weights)


def solution(mesh):
    return jax.shard_map(
        on_device,
        mesh=mesh,
        in_specs=(
            P(("dp", "mp"), None),
            P("dp", "mp"),
            P("dp", "mp"),
            P("dp", "mp"),
            P("dp", "mp"),
            P(),
            P(),
            P(),
        ),
        out_specs=(P("dp", "mp"), P("dp", "mp"), P("dp", "mp"), P(None, "mp")),
        check_vma=False,
    )
```

profile of v0, /device:TPU:1, one launch (start us, length us, event | category | flops | bytes accessed | tf_op | source)
XLA Modules:
  0.0 311.8 jit_solution(5477487466860797035)
XLA Ops:
  7.2 0.0 copy-start
  7.2 0.0 all-gather.3.cloned.1.call-start
  7.2 0.7 all-gather.3.cloned.1.call-update
  7.9 0.0 reduce-scatter.2.cloned.1.call-start
  8.0 138.1 %all-gather.3.cloned.1.call-done = bf16[2048,5120]{1,0:T(8,128)(2,1)} async-done(((bf16[128,5120]{1,0:T(8,128)(2,1)}), bf16[2048,5120]{1,0:T(8,128)(2,1)}) %all-gather.3.cloned.1.call-update) | async-done | bytes 20971536 | tf_op jit(solution)/shard_map/all_gather | solution.py:23
  146.0 0.0 copy-done
  146.0 13.9 %fusion.4 = f32[5120,320]{0,1:T(8,128)} fusion(bf16[2048,320]{0,1:T(8,128)(2,1)S(1)} %copy-done, bf16[2048,5120]{1,0:T(8,128)(2,1)} %all-gather.3.cloned.1.call-done), kind=kOutput, calls=%fused_computation.10 | convolution fusion | flops 6710886400 | bytes 28835840 | tf_op jit(solution)/shard_map/dot_general | solution.py:25
  159.9 0.0 copy-start.2
  159.9 0.0 copy-start.1
  159.9 0.0 reduce-scatter.2.cloned.1.call-update
  160.0 0.0 all-gather.5.cloned.1.call-start
  161.5 0.0 copy-done.2
  161.5 0.6 fusion.1
  162.7 40.4 %reduce-scatter.2.cloned.1.call-done = f32[640,320]{0,1:T(8,128)} async-done(((f32[5120,320]{0,1:T(8,128)}), f32[640,320]{0,1:T(8,128)}) %reduce-scatter.2.cloned.1.call-update) | async-done | bytes 819216 | tf_op jit(solution)/shard_map/reduce_scatter | solution.py:24
  203.1 0.0 copy-done.1
  203.1 4.1 %multiply_reduce_fusion = (f32[]{:T(128)}, f32[640,320]{0,1:T(8,128)S(1)}, f32[640,320]{0,1:T(8,128)}, f32[640,320]{0,1:T(8,128)}, f32[]{:T(128)}) fusion(f32[640,320]{0,1:T(8,128)S(1)} %copy-done.1, f32[]{:T(128)} %bitcast.2, f32[]{:T(128)} %bitcast.1, f32[640,320]{0,1:T(8,128)} %reduce-scatter.2.cloned.1.call-done, f32[640,320]{0,1:T(8,128)} %param.12, ...), kind=kLoop, calls=%fused_computation.3 | loop fusion | flops 3481598 | bytes 5734416 | tf_op jit(solution)/shard_map/reduce_sum | solution.py:42
  207.2 66.1 %all-reduce = (f32[]{:T(128)}, f32[]{:T(128)}) all-reduce(f32[]{:T(128)} %get-tuple-element.12, f32[]{:T(128)} %get-tuple-element.8), channel_id=1, replica_groups=mesh['dp'=8,'mp'=16] {'dp','mp'}, use_global_device_ids=true, to_apply=%region_2.0 | all-reduce | flops 2 | bytes 16 | tf_op jit(solution)/shard_map/psum | solution.py:41
  274.7 1.1 fusion.2
  275.8 0.0 all-gather.5.cloned.1.call-update
  275.8 25.6 %all-gather.5.cloned.1.call-done = bf16[5120,320]{0,1:T(8,128)(2,1)} async-done(((bf16[640,320]{0,1:T(8,128)(2,1)}), bf16[5120,320]{0,1:T(8,128)(2,1)}) %all-gather.5.cloned.1.call-update) | async-done | bytes 3276816 | tf_op jit(solution)/shard_map/all_gather | solution.py:48
  301.4 3.8 %copy.15 = bf16[5120,320]{0,1:T(8,128)(2,1)} copy(bf16[5120,320]{0,1:T(8,128)(2,1)} %all-gather.5.cloned.1.call-done) | data formatting | bytes 6553600
Async XLA Ops:
  7.2 138.9 %copy-start = (bf16[2048,320]{0,1:T(8,128)(2,1)S(1)}, bf16[2048,320]{0,1:T(8,128)(2,1)}, u32[]{:S(2)}) copy-start(bf16[2048,320]{0,1:T(8,128)(2,1)} %param.9) | copy-start | bytes 3932164
  7.2 138.9 %all-gather.3.cloned.1.call-start = ((), (), s32[]{:S(2)}) async-start(), calls=%async_computation.1 | async-start | bytes 22282240 | tf_op jit(solution)/shard_map/all_gather | solution.py:23
  7.9 195.2 %reduce-scatter.2.cloned.1.call-start = ((), (), s32[]{:S(2)}) async-start(), calls=%async_computation.2 | async-start | bytes 7372800 | tf_op jit(solution)/shard_map/reduce_scatter | solution.py:24
  159.9 1.5 copy-start.2
  159.9 43.2 %copy-start.1 = (f32[640,320]{0,1:T(8,128)S(1)}, f32[640,320]{0,1:T(8,128)}, u32[]{:S(2)}) copy-start(f32[640,320]{0,1:T(8,128)} %param.10) | copy-start | bytes 2457604
  160.0 141.4 %all-gather.5.cloned.1.call-start = ((), (), s32[]{:S(2)}) async-start(), calls=%async_computation.3 | async-start | bytes 3686400 | tf_op jit(solution)/shard_map/all_gather | solution.py:48
Sparse Core Ops, SparseCore 0:
  10.2 135.8 all-gather.2
  160.1 42.9 reduce-scatter.1
  276.0 25.3 all-gather.4
where the time goes:
time: 312 us
  waiting for transfers between devices  205 us (66%)
  blocking collectives  66.1 us (21%)
  between operations  17.2 us (6%)
  matrix products  13.9 us (4%)
  other arithmetic  5.83 us (2%)
  local copies, waits for them, and re-layouts  3.86 us (1%)
    all_gather x1, waiting for transfers between devices, on_device(): gathered = lax.all_gather(activations, 'mp', axis=0, tiled=True)  138 us
    psum x1, blocking collectives, on_device(): lax.psum((jnp.sum(master_weights * master_weights), jnp.sum(update * upda...  66.1 us
    reduce_scatter x1, waiting for transfers between devices, on_device(): lax.psum_scatter(lax.dot_general(gathered, cotangent, (((0,), (0,)), ((),...  40.4 us
    all_gather x1, waiting for transfers between devices, on_device(): lax.all_gather(new_master.astype(jnp.bfloat16), 'dp', axis=0, tiled=True)  25.6 us
    dot_general x1, matrix products, on_device(): lax.dot_general(gathered, cotangent, (((0,), (0,)), ((), ())), preferred_...  13.9 us
  transfers between devices with their start and end apart: 3, of which 3 were waited for; matrix products, arithmetic and copies ran while one was open for 0% of the time, Pallas kernels for 0%

commit v1 on v0

--- a/solution.py
+++ b/solution.py
@@ -45,7 +45,12 @@
     picked = jnp.arange(language_rates.shape[0], dtype=jnp.int32) == language_ids[0]
     rate = base_rate * jnp.sum(jnp.where(picked, language_rates, jnp.float32(0.0)))
     new_master = master_weights - rate * trust * update
-    new_weights = lax.all_gather(new_master.astype(jnp.bfloat16), "dp", axis=0, tiled=True)
+    new_weights = jnp.concatenate(
+        lax.all_to_all(
+            jnp.stack([new_master.astype(jnp.bfloat16)] * lax.axis_size("dp")), "dp", 0, 0
+        ),
+        axis=0,
+    )
     return (new_master, new_first, new_second, new_weights)
 
 

time: 312 us -> 328 us (1.051)
  blocking collectives: 66.1 us -> 109 us
  waiting for transfers between devices: 205 us -> 179 us
    all_to_all x0 -> x1, blocking collectives: none -> 42.9 us  [on_device(): lax.all_to_all(jnp.stack([new_master.astype(jnp.bfloat16)] * lax.axis_siz...]
    all_gather x1 -> x0, waiting for transfers between devices: 25.6 us -> none  [on_device(): lax.all_gather(new_master.astype(jnp.bfloat16), 'dp', axis=0, tiled=True)]
    unnamed x7 -> x6, local copies, waits for them, and re-layouts: 3.86 us -> 0.02 us
  transfers between devices with their start and end apart: 3 -> 2, of which waited for: 3 -> 2; matrix products, arithmetic and copies ran while one was open for 0% -> 0% of each run, Pallas kernels for 0% -> 0%
where the time goes in v1:
time: 328 us
  waiting for transfers between devices  179 us (55%)
  blocking collectives  109 us (33%)
  between operations  17.6 us (5%)
  matrix products  13.9 us (4%)
  other arithmetic  5.7 us (2%)
    all_gather x1, waiting for transfers between devices, on_device(): gathered = lax.all_gather(activations, 'mp', axis=0, tiled=True)  138 us
    psum x1, blocking collectives, on_device(): lax.psum((jnp.sum(master_weights * master_weights), jnp.sum(update * upda...  66.1 us
    all_to_all x1, blocking collectives, on_device(): lax.all_to_all(jnp.stack([new_master.astype(jnp.bfloat16)] * lax.axis_siz...  42.9 us
    reduce_scatter x1, waiting for transfers between devices, on_device(): lax.psum_scatter(lax.dot_general(gathered, cotangent, (((0,), (0,)), ((),...  40.4 us
    dot_general x1, matrix products, on_device(): lax.dot_general(gathered, cotangent, (((0,), (0,)), ((), ())), preferred_...  13.9 us
  transfers between devices with their start and end apart: 2, of which 2 were waited for; matrix products, arithmetic and copies ran while one was open for 0% of the time, Pallas kernels for 0%

profile of v1, /device:TPU:1, one launch (start us, length us, event | category | flops | bytes accessed | tf_op | source)
XLA Modules:
  0.0 327.9 jit_solution(2286281235317851598)
XLA Ops:
  7.2 0.0 copy-start
  7.2 0.0 all-gather.2.cloned.1.call-start
  7.2 0.7 all-gather.2.cloned.1.call-update
  7.9 0.0 reduce-scatter.2.cloned.1.call-start
  8.0 138.1 %all-gather.2.cloned.1.call-done = bf16[2048,5120]{1,0:T(8,128)(2,1)} async-done(((bf16[128,5120]{1,0:T(8,128)(2,1)}), bf16[2048,5120]{1,0:T(8,128)(2,1)}) %all-gather.2.cloned.1.call-update) | async-done | bytes 20971536 | tf_op jit(solution)/shard_map/all_gather | solution.py:23
  146.0 0.0 copy-done
  146.1 13.9 %fusion.4 = f32[5120,320]{0,1:T(8,128)} fusion(bf16[2048,320]{0,1:T(8,128)(2,1)S(1)} %copy-done, bf16[2048,5120]{1,0:T(8,128)(2,1)} %all-gather.2.cloned.1.call-done), kind=kOutput, calls=%fused_computation.10 | convolution fusion | flops 6710886400 | bytes 28835840 | tf_op jit(solution)/shard_map/dot_general | solution.py:25
  159.9 0.0 copy-start.2
  159.9 0.0 copy-start.1
  159.9 0.0 reduce-scatter.2.cloned.1.call-update
  161.4 0.0 copy-done.2
  161.4 0.6 fusion.1
  162.7 40.4 %reduce-scatter.2.cloned.1.call-done = f32[640,320]{0,1:T(8,128)} async-done(((f32[5120,320]{0,1:T(8,128)}), f32[640,320]{0,1:T(8,128)}) %reduce-scatter.2.cloned.1.call-update) | async-done | bytes 819216 | tf_op jit(solution)/shard_map/reduce_scatter | solution.py:24
  203.1 0.0 copy-done.1
  203.1 4.1 %multiply_reduce_fusion = (f32[]{:T(128)}, f32[640,320]{0,1:T(8,128)S(1)}, f32[640,320]{0,1:T(8,128)}, f32[640,320]{0,1:T(8,128)}, f32[]{:T(128)}) fusion(f32[640,320]{0,1:T(8,128)S(1)} %copy-done.1, f32[]{:T(128)} %bitcast.2, f32[]{:T(128)} %bitcast.1, f32[640,320]{0,1:T(8,128)} %reduce-scatter.2.cloned.1.call-done, f32[640,320]{0,1:T(8,128)} %param.12, ...), kind=kLoop, calls=%fused_computation.3 | loop fusion | flops 3481598 | bytes 5734416 | tf_op jit(solution)/shard_map/reduce_sum | solution.py:42
  207.2 66.1 %all-reduce = (f32[]{:T(128)}, f32[]{:T(128)}) all-reduce(f32[]{:T(128)} %get-tuple-element.12, f32[]{:T(128)} %get-tuple-element.8), channel_id=1, replica_groups=mesh['dp'=8,'mp'=16] {'dp','mp'}, use_global_device_ids=true, to_apply=%region_2.0 | all-reduce | flops 2 | bytes 16 | tf_op jit(solution)/shard_map/psum | solution.py:41
  274.7 1.0 fusion.2
  275.7 0.3 stack.2
  275.9 42.9 %all_to_all.5 = bf16[8,640,320]{1,2,0:T(8,128)(2,1)S(1)} all-to-all(bf16[8,640,320]{1,2,0:T(8,128)(2,1)S(1)} %stack.2), channel_id=1, replica_groups=mesh['dp'=8,'mp'=16] {'dp'}, dimensions={0} | all-to-all | bytes 6553600 | tf_op jit(solution)/shard_map/all_to_all | solution.py:49
  318.8 2.2 copy.13
Async XLA Ops:
  7.2 138.9 %copy-start = (bf16[2048,320]{0,1:T(8,128)(2,1)S(1)}, bf16[2048,320]{0,1:T(8,128)(2,1)}, u32[]{:S(2)}) copy-start(bf16[2048,320]{0,1:T(8,128)(2,1)} %param.9) | copy-start | bytes 3932164
  7.2 138.9 %all-gather.2.cloned.1.call-start = ((), (), s32[]{:S(2)}) async-start(), calls=%async_computation.2 | async-start | bytes 22282240 | tf_op jit(solution)/shard_map/all_gather | solution.py:23
  7.9 195.2 %reduce-scatter.2.cloned.1.call-start = ((), (), s32[]{:S(2)}) async-start(), calls=%async_computation.3 | async-start | bytes 7372800 | tf_op jit(solution)/shard_map/reduce_scatter | solution.py:24
  159.9 1.5 copy-start.2
  159.9 43.2 %copy-start.1 = (f32[640,320]{0,1:T(8,128)S(1)}, f32[640,320]{0,1:T(8,128)}, u32[]{:S(2)}) copy-start(f32[640,320]{0,1:T(8,128)} %param.10) | copy-start | bytes 2457604
Sparse Core Ops, SparseCore 0:
  10.2 135.7 all-gather.1
  160.1 42.9 reduce-scatter.1
